TPU v7x, 256 devices: a whole 4x4x8 slice. The times are simulated.
256 devices in a mesh: date: 8 (over x, y_hi), path: 32 (over z, y_lo, core).
Axes of the slice: x: 4, y: 4 (y_hi: 2, y_lo: 2; y = y_hi * 2 + y_lo), z: 8, core: 2. Of those that a mesh axis runs over, the one named last changes fastest.
Arguments:
- factors: bfloat16 [64, 16, 131072], P('date', None, 'path'), may hold values from -10 to 10
- cashflows: bfloat16 [64, 64, 131072], P('date', None, 'path'), may hold values from -12 to 12
- frequency: bfloat16 [128, 16], replicated, may hold values from -1.5 to 1.5
- phases: float32 [128], replicated, may hold values from -3.140625 to 3.140625
- margin_lag: int32 [64], replicated, may hold values from 1 to 2
- thresholds: int32 [64], replicated, may hold values from 0 to 149
- transfer_min: int32 [64], replicated, may hold values from 0 to 59
Outputs:
- exposure: bfloat16 [64, 64, 131072], P('date', None, 'path')
- profile: float32 [64, 64], P('date')
All inputs are finite; a program needn't handle non-finite values.
Results may differ from a plain program's by a relative error of at most 0.0058.
Values may be sent and summed in bfloat16 or wider, within the bound.
No kernel may reach another device: no remote copies, remote signals or barrier semaphores. Data moves between devices by JAX's collectives and lax.ppermute only.
A program may use at most 128 MiB of HBM per device.

v0:
```python
import jax
import jax.numpy as jnp
from jax import lax
from jax.sharding import PartitionSpec as P

LAG_MAX = 2
ridge_weight = 0.05
root_two = 1.4142135623730951


def shifted_2(value, axis, by):
    length = lax.axis_size(axis)
    pairs = [(i, i + by) for i in range(length) if 0 <= i + by < length]
    return lax.ppermute(value, axis, pairs)


def packed_total(arrays, axis):
    ends = [0]
    for a in arrays:
        ends.append(ends[-1] + a.size)
    total = lax.psum(jnp.concatenate([a.ravel() for a in arrays]), axis)
    return tuple((total[b:e].reshape(a.shape) for a, b, e in zip(arrays, ends, ends[1:])))


def from_everyone(value, axis):
    length = lax.axis_size(axis)
    return lax.all_to_all(
        jnp.broadcast_to(value[None], (length, *value.shape)), axis, 0, 0, tiled=True
    )


def over_copies(value, axis):
    return from_everyone(value, axis).sum(axis=0)


def featurize(frequency, phases, factors):
    angles = jnp.einsum("kr,trp->tkp", frequency, factors, preferred_element_type=jnp.float32)
    angles = angles + phases[None, :, None]
    return (root_two * jnp.cos(angles)).astype(jnp.bfloat16)


def regress(gram_sum, right_sum, paths_all):
    system = (
        gram_sum / paths_all + ridge_weight * jnp.eye(gram_sum.shape[-1], dtype=jnp.float32)[None]
    )
    factor = lax.linalg.cholesky(system)
    solved = lax.linalg.triangular_solve(factor, right_sum / paths_all, left_side=True, lower=True)
    solved = lax.linalg.triangular_solve(
        factor, solved, left_side=True, lower=True, transpose_a=True
    )
    return solved.astype(jnp.bfloat16)


def fitted(coefficients, features):
    return jnp.einsum(
        "tkn,tkp->tnp", coefficients, features, preferred_element_type=jnp.float32
    ).astype(jnp.bfloat16)


def local(factors, cashflows, frequency, phases, margin_lag, thresholds, transfer_min):
    prior_factors = shifted_2(factors[-LAG_MAX:], "date", 1)
    features = featurize(frequency, phases, factors)
    gram_sum = jnp.einsum("tkp,tjp->tkj", features, features, preferred_element_type=jnp.float32)
    right_sum = jnp.einsum("tkp,tnp->tkn", features, cashflows, preferred_element_type=jnp.float32)
    gram_sum, right_sum = packed_total((gram_sum, right_sum), "path")
    paths_all = features.shape[2] * lax.axis_size("path")
    coefficients = regress(gram_sum, right_sum, paths_all)
    values = fitted(coefficients, features)
    prior_coefs = shifted_2(coefficients[-LAG_MAX:], "date", 1)
    prior_values = fitted(prior_coefs, featurize(frequency, phases, prior_factors))
    joined = jnp.concatenate([prior_values, values], axis=0)
    dates_here = values.shape[0]
    lagged = jnp.zeros(values.shape, jnp.float32)
    for lag_value in range(1, LAG_MAX + 1):
        shifted = joined[LAG_MAX - lag_value : LAG_MAX - lag_value + dates_here].astype(jnp.float32)
        lagged = jnp.where((margin_lag == lag_value)[None, :, None], shifted, lagged)
    offset = (thresholds + transfer_min).astype(jnp.float32) / 100.0
    collateral = jnp.maximum(lagged - offset[None, :, None], 0.0)
    exposure = jnp.maximum(values.astype(jnp.float32) - collateral, 0.0)
    profile = over_copies(jnp.sum(exposure, axis=2), "path") / paths_all
    return (exposure.astype(jnp.bfloat16), profile)


def solution(mesh):
    return jax.shard_map(
        local,
        mesh=mesh,
        in_specs=(P("date", None, "path"), P("date", None, "path"), P(), P(), P(), P(), P()),
        out_specs=(P("date", None, "path"), P("date", None)),
        check_vma=False,
    )
```

profile of v0, /device:TPU:1, one launch (start us, length us, event | category | flops | bytes accessed | tf_op | source)
XLA Modules:
  0.0 543.0 jit_solution(3618707060904881406)
XLA Ops:
  7.2 0.0 copy-start
  7.2 0.0 all-reduce.2.cloned.1.call-start
  7.2 0.6 copy-done
  7.9 58.2 %multiply_convert_fusion = bf16[8,4096,128]{2,1,0:T(8,128)(2,1)S(1)} fusion(bf16[8,16,4096]{2,1,0:T(8,128)(2,1)} %param.7, f32[128]{0:T(128)} %param.10, bf16[128,16]{0,1:T(8,128)(2,1)S(1)} %copy-done), kind=kOutput, calls=%fused_computation | convolution fusion | flops 146800640 | bytes 9441792 | tf_op jit(solution)/shard_map/kr,trp->tkp/dot_general | solution.py:37
  66.1 0.0 copy-start.1
  66.1 2.5 fusion.13
  68.6 0.7 copy-done.1
  69.3 0.0 copy-start.2
  69.3 0.0 copy-start.3
  69.3 0.0 copy-start.4
  69.3 4.8 fusion.14
  74.2 0.1 reshape.58
  74.3 0.9 pad_maximum_fusion.1
  75.2 0.0 all-reduce.2.cloned.1.call-update
  75.3 1.0 slice.49
  76.2 6.1 %collective-permute-start.1 = (bf16[2,16,4096]{2,1,0:T(8,128)(2,1)S(1)}, bf16[2,16,4096]{2,1,0:T(8,128)(2,1)S(1)}, u32[]{:S(2)}, u32[]{:S(2)}) collective-permute-start(bf16[2,16,4096]{2,1,0:T(8,128)(2,1)S(1)} %slice.49), channel_id=1, source_target_pairs={{0,32},{32,64},{64,96},{96,128},{128,160},{160,192},{192,224},{1,3... | collective-permute-start | bytes 786440 | tf_op jit(solution)/shard_map/ppermute | solution.py:14
  82.4 0.1 copy.21
  82.5 0.0 copy-done.2
  82.6 0.0 copy-done.3
  82.6 0.0 copy-done.4
  82.6 222.5 %all-reduce.2.cloned.1.call-done = f32[196608]{0:T(1024)} async-done(((f32[196608]{0:T(1024)}), f32[196608]{0:T(1024)}) %all-reduce.2.cloned.1.call-update) | async-done | bytes 786448 | tf_op jit(solution)/shard_map/psum | solution.py:21
  305.1 1.1 slice_multiply_fusion
  306.2 0.2 copy.22
  306.4 0.2 copy.23
  306.6 0.1 fusion.7
  306.7 93.8 %custom-call.8 = f32[8,128,128]{2,1,0:T(8,128)S(1)} custom-call(f32[8,128,128]{2,1,0:T(8,128)S(1)} %fusion.7), custom_call_target="Cholesky" | custom-call | tf_op jit(solution)/shard_map/cholesky | solution.py:46
  400.5 0.1 select_reduce_fusion
  400.5 0.1 compare_reduce_fusion
  400.7 0.1 select_bitcast_fusion
  400.8 0.0 copy-start.5
  400.8 78.6 %custom-call.9 = f32[8,1,128,128]{2,3,1,0:T(8,128)S(1)} custom-call(f32[8,1,128,128]{3,2,1,0:T(8,128)S(1)} %select_bitcast_fusion), custom_call_target="InvertDiagBlocksLowerTriangular" | custom-call | tf_op jit(solution)/shard_map/triangular_solve | solution.py:48
  479.4 1.0 slice_multiply_fusion.1
  480.4 0.1 div.41
  480.5 1.0 fusion.5
  481.6 1.1 convolution_convert_fusion.2
  482.7 4.5 collective-permute-start
  487.2 8.4 %convolution_convert_fusion = bf16[8,64,4096]{2,1,0:T(8,128)(2,1)} fusion(bf16[8,128,64]{1,2,0:T(8,128)(2,1)S(1)} %convolution_convert_fusion.2, bf16[8,4096,128]{2,1,0:T(8,128)(2,1)} %copy-done.1), kind=kOutput, calls=%fused_computation.2 | convolution fusion | flops 538968064 | bytes 12713984 | tf_op jit(solution)/shard_map/tkn,tkp->tnp/dot_general | solution.py:55
  495.6 0.0 collective-permute-done.1
  495.6 0.0 collective-permute-done
  495.6 0.0 copy-done.5
  495.6 14.6 %convolution_convert_fusion.1 = bf16[2,64,4096]{2,1,0:T(8,128)(2,1)S(1)} fusion(bf16[2,128,64]{1,2,0:T(8,128)(2,1)S(1)} %collective-permute-done, bf16[2,16,4096]{2,1,0:T(8,128)(2,1)S(1)} %collective-permute-done.1, f32[128]{0:T(128)S(1)} %copy-done.5, bf16[128,16]{0,1:T(8,128)(2,1)S(1)} %copy-done), kind=kOutput, calls=%fused_computation.9 | convolution fusion | flops 171442176 | bytes 1348096 | tf_op jit(solution)/shard_map/tkn,tkp->tnp/dot_general | solution.py:55
  510.2 7.9 %fusion.12 = (f32[8,64]{1,0:T(8,128)S(1)}, bf16[8,64,4096]{2,1,0:T(8,128)(2,1)}) fusion(f32[64]{0:T(128)S(1)} %convert_multiply_fusion, bf16[8,64,4096]{2,1,0:T(8,128)(2,1)} %convolution_convert_fusion, bf16[2,64,4096]{2,1,0:T(8,128)(2,1)S(1)} %convolution_convert_fusion.1, pred[64]{0:T(512)(128)(4,1)S(1)} %get-tuple-element.5, ...), kind=kLoop, calls=%fused_computation.35 | loop fusion | flops 27262464 | bytes 9439616 | tf_op jit(solution)/shard_map/reduce_sum | solution.py:80
  518.1 0.1 reshape.60
  518.2 15.6 %all_to_all.5 = f32[32,1,512]{2,1,0:T(1,128)S(1)} all-to-all(f32[32,1,512]{2,1,0:T(1,128)S(1)} %reshape.60), channel_id=1, replica_groups=mesh['date'=8,'path'=32] {'path'}, dimensions={0} | all-to-all | bytes 131072 | tf_op jit(solution)/shard_map/all_to_all | solution.py:27
  533.9 0.5 broadcast.86
  534.4 0.8 reduce.4
  535.2 0.1 reshape.61
  535.3 0.6 broadcast_multiply_fusion
  (9 shorter events, 0.1 us)
Async XLA Ops:
  7.2 0.7 copy-start
  7.2 297.9 %all-reduce.2.cloned.1.call-start = ((), (), s32[]{:S(2)}) async-start(), calls=%async_computation.1 | async-start | bytes 1572864 | tf_op jit(solution)/shard_map/psum | solution.py:21
  66.1 3.2 copy-start.1
  69.3 13.2 %copy-start.2 = (s32[64]{0:T(128)S(1)}, s32[64]{0:T(128)}, u32[]{:S(2)}) copy-start(s32[64]{0:T(128)} %param.11) | copy-start | bytes 772
  69.3 13.2 %copy-start.3 = (s32[64]{0:T(128)S(1)}, s32[64]{0:T(128)}, u32[]{:S(2)}) copy-start(s32[64]{0:T(128)} %param.12) | copy-start | bytes 772
  69.3 13.3 %copy-start.4 = (s32[64]{0:T(128)S(1)}, s32[64]{0:T(128)}, u32[]{:S(2)}) copy-start(s32[64]{0:T(128)} %param.13) | copy-start | bytes 772
  76.2 419.4 %collective-permute-start.1 = (bf16[2,16,4096]{2,1,0:T(8,128)(2,1)S(1)}, bf16[2,16,4096]{2,1,0:T(8,128)(2,1)S(1)}, u32[]{:S(2)}, u32[]{:S(2)}) collective-permute-start(bf16[2,16,4096]{2,1,0:T(8,128)(2,1)S(1)} %slice.49), channel_id=1, source_target_pairs={{0,32},{32,64},{64,96},{96,128},{128,160},{160,192},{192,224},{1,3... | collective-permute-start | bytes 786440 | tf_op jit(solution)/shard_map/ppermute | solution.py:14
  400.8 94.8 %copy-start.5 = (f32[128]{0:T(128)S(1)}, f32[128]{0:T(128)}, u32[]{:S(2)}) copy-start(f32[128]{0:T(128)} %param.10) | copy-start | bytes 1540
  482.7 12.9 %collective-permute-start = (bf16[2,128,64]{1,2,0:T(8,128)(2,1)S(1)}, bf16[2,128,64]{1,2,0:T(8,128)(2,1)S(1)}, u32[]{:S(2)}, u32[]{:S(2)}) collective-permute-start(bf16[2,128,64]{1,2,0:T(8,128)(2,1)S(1)} %slice.54), channel_id=1, source_target_pairs={{0,32},{32,64},{64,96},{96,128},{128,160},{160,192},{192,224},{1,3... | collective-permute-start | bytes 98312 | tf_op jit(solution)/shard_map/ppermute | solution.py:14
Sparse Core Ops, SparseCore 0:
  75.4 229.6 all-reduce.1
where the time goes:
time: 550 us; the launch traced here: 543 us
  waiting for transfers between devices  223 us (41%)
  other arithmetic  185 us (34%)
  matrix products  90.7 us (16%)
  blocking collectives  15.6 us (3%)
  between operations  14.5 us (3%)
  starting transfers between devices  10.7 us (2%)
    psum x1, waiting for transfers between devices, packed_total(): total = lax.psum(jnp.concatenate([a.ravel() for a in arrays]), axis)  222 us
    another operation x4, other arithmetic, regress(): factor = lax.linalg.cholesky(system)  94 us
    another operation x3, other arithmetic, regress(): lax.linalg.triangular_solve(factor, solved, left_side=True, lower=True, t...  78.7 us
    dot_general x1, matrix products, featurize(): jnp.einsum('kr,trp->tkp', frequency, factors, preferred_element_type=jnp....  58.2 us
    dot_general x2, matrix products, fitted(): jnp.einsum('tkn,tkp->tnp', coefficients, features, preferred_element_type...  23 us
    all_to_all x1, blocking collectives, from_everyone(): lax.all_to_all(jnp.broadcast_to(value[None], (length, *value.shape)), axi...  15.6 us
  transfers between devices with their start and end apart: 3, of which 1 were waited for; matrix products, arithmetic and copies ran while one was open for 34% of the time, Pallas kernels for 0%

commit v1 on v0

--- a/solution.py
+++ b/solution.py
@@ -18,7 +18,7 @@
     ends = [0]
     for a in arrays:
         ends.append(ends[-1] + a.size)
-    total = lax.psum(jnp.concatenate([a.ravel() for a in arrays]), axis)
+    total = jnp.sum(lax.all_gather(jnp.concatenate([a.ravel() for a in arrays]), axis), axis=0)
     return tuple((total[b:e].reshape(a.shape) for a, b, e in zip(arrays, ends, ends[1:])))
 
 

time: 550 us -> 503 us (0.915)
  waiting for transfers between devices: 223 us -> 139 us
  local copies, waits for them, and re-layouts: 3.86 us -> 30.1 us
  other arithmetic: 185 us -> 195 us
    psum x1 -> x0, waiting for transfers between devices: 222 us -> none  [packed_total(): total = lax.psum(jnp.concatenate([a.ravel() for a in arrays]), axis)]
    all_gather x0 -> x1, waiting for transfers between devices: none -> 139 us  [packed_total(): lax.all_gather(jnp.concatenate([a.ravel() for a in arrays]), axis)]
    all_gather x0 -> x1, local copies, waits for them, and re-layouts: none -> 26.2 us  [packed_total(): lax.all_gather(jnp.concatenate([a.ravel() for a in arrays]), axis)]
    reduce_sum x0 -> x1, other arithmetic: none -> 12.3 us  [packed_total(): jnp.sum(lax.all_gather(jnp.concatenate([a.ravel() for a in arrays]), axis...]
  transfers between devices with their start and end apart: 3 -> 3, of which waited for: 1 -> 1; matrix products, arithmetic and copies ran while one was open for 34% -> 45% of each run, Pallas kernels for 0% -> 0%
where the time goes in v1:
time: 503 us; the launch traced here: 496 us
  other arithmetic  195 us (39%)
  waiting for transfers between devices  139 us (28%)
  matrix products  90.6 us (18%)
  local copies, waits for them, and re-layouts  30.1 us (6%)
  blocking collectives  14.9 us (3%)
  between operations  14.5 us (3%)
  starting transfers between devices  11 us (2%)
    all_gather x1, waiting for transfers between devices, packed_total(): lax.all_gather(jnp.concatenate([a.ravel() for a in arrays]), axis)  139 us
    another operation x4, other arithmetic, regress(): factor = lax.linalg.cholesky(system)  94 us
    another operation x3, other arithmetic, regress(): lax.linalg.triangular_solve(factor, solved, left_side=True, lower=True, t...  78.7 us
    dot_general x1, matrix products, featurize(): jnp.einsum('kr,trp->tkp', frequency, factors, preferred_element_type=jnp....  58.2 us
    all_gather x1, local copies, waits for them, and re-layouts, packed_total(): lax.all_gather(jnp.concatenate([a.ravel() for a in arrays]), axis)  26.2 us
    dot_general x2, matrix products, fitted(): jnp.einsum('tkn,tkp->tnp', coefficients, features, preferred_element_type...  23 us
    all_to_all x1, blocking collectives, from_everyone(): lax.all_to_all(jnp.broadcast_to(value[None], (length, *value.shape)), axi...  14.9 us
    reduce_sum x1, other arithmetic, packed_total(): jnp.sum(lax.all_gather(jnp.concatenate([a.ravel() for a in arrays]), axis...  12.3 us
  transfers between devices with their start and end apart: 3, of which 1 were waited for; matrix products, arithmetic and copies ran while one was open for 45% of the time, Pallas kernels for 0%

profile of v1, /device:TPU:1, one launch (start us, length us, event | category | flops | bytes accessed | tf_op | source)
XLA Modules:
  0.0 495.5 jit_solution(1922192161066481538)
XLA Ops:
  7.2 0.0 copy-start
  7.2 0.0 all-gather.3.cloned.1.call-start
  7.2 0.6 copy-done
  7.9 58.2 %multiply_convert_fusion = bf16[8,4096,128]{2,1,0:T(8,128)(2,1)S(1)} fusion(bf16[8,16,4096]{2,1,0:T(8,128)(2,1)} %param.7, f32[128]{0:T(128)} %param.10, bf16[128,16]{0,1:T(8,128)(2,1)S(1)} %copy-done), kind=kOutput, calls=%fused_computation | convolution fusion | flops 146800640 | bytes 9441792 | tf_op jit(solution)/shard_map/kr,trp->tkp/dot_general | solution.py:37
  66.1 0.0 copy-start.1
  66.1 2.5 fusion.13
  68.6 0.7 copy-done.1
  69.3 0.0 copy-start.2
  69.3 0.0 copy-start.3
  69.3 0.0 copy-start.4
  69.3 4.8 fusion.14
  74.1 0.1 reshape.58
  74.3 0.9 pad_maximum_fusion.1
  75.2 0.0 all-gather.3.cloned.1.call-update
  75.3 1.0 slice.49
  76.2 6.1 %collective-permute-start.1 = (bf16[2,16,4096]{2,1,0:T(8,128)(2,1)S(1)}, bf16[2,16,4096]{2,1,0:T(8,128)(2,1)S(1)}, u32[]{:S(2)}, u32[]{:S(2)}) collective-permute-start(bf16[2,16,4096]{2,1,0:T(8,128)(2,1)S(1)} %slice.49), channel_id=1, source_target_pairs={{0,32},{32,64},{64,96},{96,128},{128,160},{160,192},{192,224},{1,3... | collective-permute-start | bytes 786440 | tf_op jit(solution)/shard_map/ppermute | solution.py:14
  82.4 0.1 copy.29
  82.5 0.0 copy-done.2
  82.5 0.0 copy-done.3
  82.6 0.0 copy-done.4
  82.6 139.0 %all-gather.3.cloned.1.call-done = f32[6291456]{0:T(1024)} async-done(((f32[196608]{0:T(1024)}), f32[6291456]{0:T(1024)}) %all-gather.3.cloned.1.call-update) | async-done | bytes 25165840 | tf_op jit(solution)/shard_map/all_gather | solution.py:21
  221.6 26.2 %reshape.59 = f32[32,196608]{1,0:T(8,128)} reshape(f32[6291456]{0:T(1024)} %all-gather.3.cloned.1.call-done) | data formatting | bytes 50331648 | tf_op jit(solution)/shard_map/all_gather | solution.py:21
  247.8 12.3 %reduce_sum.27 = f32[196608]{0:T(1024)S(1)} reduce(f32[32,196608]{1,0:T(8,128)} %reshape.59, f32[]{:T(128)} %constant.48.clone.1), dimensions={0}, to_apply=%region_0.0 | reduce | flops 6094848 | bytes 25952260 | tf_op jit(solution)/shard_map/reduce_sum | solution.py:21
  260.3 0.2 copy.30
  260.5 0.2 copy.31
  260.7 0.1 fusion.7
  260.8 93.8 %custom-call.8 = f32[8,128,128]{2,1,0:T(8,128)S(1)} custom-call(f32[8,128,128]{2,1,0:T(8,128)S(1)} %fusion.7), custom_call_target="Cholesky" | custom-call | tf_op jit(solution)/shard_map/cholesky | solution.py:46
  354.6 0.1 select_reduce_fusion
  354.6 0.1 compare_reduce_fusion
  354.7 0.0 copy-start.5
  354.7 0.1 select_bitcast_fusion
  354.9 78.6 %custom-call.9 = f32[8,1,128,128]{2,3,1,0:T(8,128)S(1)} custom-call(f32[8,1,128,128]{3,2,1,0:T(8,128)S(1)} %select_bitcast_fusion), custom_call_target="InvertDiagBlocksLowerTriangular" | custom-call | tf_op jit(solution)/shard_map/triangular_solve | solution.py:48
  433.5 0.1 div.41
  433.6 1.0 fusion.5
  434.7 1.1 convolution_convert_fusion.2
  435.8 4.8 collective-permute-start
  440.6 8.3 %convolution_convert_fusion = bf16[8,64,4096]{2,1,0:T(8,128)(2,1)} fusion(bf16[8,128,64]{1,2,0:T(8,128)(2,1)S(1)} %convolution_convert_fusion.2, bf16[8,4096,128]{2,1,0:T(8,128)(2,1)} %copy-done.1), kind=kOutput, calls=%fused_computation.2 | convolution fusion | flops 538968064 | bytes 12713984 | tf_op jit(solution)/shard_map/tkn,tkp->tnp/dot_general | solution.py:55
  448.9 0.0 collective-permute-done.1
  448.9 0.0 collective-permute-done
  448.9 0.0 copy-done.5
  448.9 14.6 %convolution_convert_fusion.1 = bf16[2,64,4096]{2,1,0:T(8,128)(2,1)S(1)} fusion(bf16[2,128,64]{1,2,0:T(8,128)(2,1)S(1)} %collective-permute-done, bf16[2,16,4096]{2,1,0:T(8,128)(2,1)S(1)} %collective-permute-done.1, f32[128]{0:T(128)S(1)} %copy-done.5, bf16[128,16]{0,1:T(8,128)(2,1)S(1)} %copy-done), kind=kOutput, calls=%fused_computation.9 | convolution fusion | flops 171442176 | bytes 1348096 | tf_op jit(solution)/shard_map/tkn,tkp->tnp/dot_general | solution.py:55
  463.6 7.8 %fusion.12 = (f32[8,64]{1,0:T(8,128)S(1)}, bf16[8,64,4096]{2,1,0:T(8,128)(2,1)}) fusion(f32[64]{0:T(128)S(1)} %convert_multiply_fusion, bf16[8,64,4096]{2,1,0:T(8,128)(2,1)} %convolution_convert_fusion, bf16[2,64,4096]{2,1,0:T(8,128)(2,1)S(1)} %convolution_convert_fusion.1, pred[64]{0:T(512)(128)(4,1)S(1)} %get-tuple-element.5, ...), kind=kLoop, calls=%fused_computation.35 | loop fusion | flops 27262464 | bytes 9439616 | tf_op jit(solution)/shard_map/reduce_sum | solution.py:80
  471.4 0.1 reshape.61
  471.5 14.9 %all_to_all.5 = f32[32,1,512]{2,1,0:T(1,128)S(1)} all-to-all(f32[32,1,512]{2,1,0:T(1,128)S(1)} %reshape.61), channel_id=1, replica_groups=mesh['date'=8,'path'=32] {'path'}, dimensions={0} | all-to-all | bytes 131072 | tf_op jit(solution)/shard_map/all_to_all | solution.py:27
  486.4 0.5 broadcast.86
  486.9 0.8 reduce.4
  487.7 0.1 reshape.62
  487.9 0.6 broadcast_multiply_fusion
  (11 shorter events, 0.2 us)
Async XLA Ops:
  7.2 0.7 copy-start
  7.2 214.4 %all-gather.3.cloned.1.call-start = ((), (), s32[]{:S(2)}) async-start(), calls=%async_computation.1 | async-start | bytes 25952256 | tf_op jit(solution)/shard_map/all_gather | solution.py:21
  66.1 3.2 copy-start.1
  69.3 13.2 %copy-start.2 = (s32[64]{0:T(128)S(1)}, s32[64]{0:T(128)}, u32[]{:S(2)}) copy-start(s32[64]{0:T(128)} %param.11) | copy-start | bytes 772
  69.3 13.2 %copy-start.3 = (s32[64]{0:T(128)S(1)}, s32[64]{0:T(128)}, u32[]{:S(2)}) copy-start(s32[64]{0:T(128)} %param.12) | copy-start | bytes 772
  69.3 13.3 %copy-start.4 = (s32[64]{0:T(128)S(1)}, s32[64]{0:T(128)}, u32[]{:S(2)}) copy-start(s32[64]{0:T(128)} %param.13) | copy-start | bytes 772
  76.2 372.7 %collective-permute-start.1 = (bf16[2,16,4096]{2,1,0:T(8,128)(2,1)S(1)}, bf16[2,16,4096]{2,1,0:T(8,128)(2,1)S(1)}, u32[]{:S(2)}, u32[]{:S(2)}) collective-permute-start(bf16[2,16,4096]{2,1,0:T(8,128)(2,1)S(1)} %slice.49), channel_id=1, source_target_pairs={{0,32},{32,64},{64,96},{96,128},{128,160},{160,192},{192,224},{1,3... | collective-permute-start | bytes 786440 | tf_op jit(solution)/shard_map/ppermute | solution.py:14
  354.7 94.2 %copy-start.5 = (f32[128]{0:T(128)S(1)}, f32[128]{0:T(128)}, u32[]{:S(2)}) copy-start(f32[128]{0:T(128)} %param.10) | copy-start | bytes 1540
  435.8 13.1 %collective-permute-start = (bf16[2,128,64]{1,2,0:T(8,128)(2,1)S(1)}, bf16[2,128,64]{1,2,0:T(8,128)(2,1)S(1)}, u32[]{:S(2)}, u32[]{:S(2)}) collective-permute-start(bf16[2,128,64]{1,2,0:T(8,128)(2,1)S(1)} %slice.54), channel_id=1, source_target_pairs={{0,32},{32,64},{64,96},{96,128},{128,160},{160,192},{192,224},{1,3... | collective-permute-start | bytes 98312 | tf_op jit(solution)/shard_map/ppermute | solution.py:14
Sparse Core Ops, SparseCore 0:
  75.4 146.1 all-gather.2
